TPU v7x, 128 devices: a whole 4x4x4 slice. The times are simulated.
128 devices in a mesh: section: 2 (over x_lo), dp: 16 (over x_hi, y, core), mp: 4 (over z).
Axes of the slice: x: 4 (x_hi: 2, x_lo: 2; x = x_hi * 2 + x_lo), y: 4, z: 4, core: 2. Of those that a mesh axis runs over, the one named last changes fastest.
Arguments:
- hidden: bfloat16 [2, 16, 256, 5120], P('section', 'dp'), may hold values from -6 to 6
- gain: float32 [2, 5120], P('section'), may hold values from 0.5 to 2
- w_first: bfloat16 [2, 5120, 2560], P('section', 'dp', 'mp'), may hold values from -0.078125 to 0.078125
- w_second: bfloat16 [2, 5120, 2560], P('section', 'dp', 'mp'), may hold values from -0.078125 to 0.078125
- lengths: int32 [16, 2], P('dp'), may hold values from 32 to 256, as said below
- cotangent: bfloat16 [2, 16, 256, 5120], P('section', 'dp'), may hold values from -6 to 6
Outputs:
- result: bfloat16 [2, 16, 256, 5120], P('section', 'dp')
- d_hidden: bfloat16 [2, 16, 256, 5120], P('section', 'dp')
- d_gain: float32 [2, 5120], P('section', 'dp')
- d_first: float32 [2, 5120, 2560], P('section', 'dp', 'mp')
- d_second: float32 [2, 5120, 2560], P('section', 'dp', 'mp')
Inputs may be any that keep to these rules, and one draw needn't show every extreme that they name: `lengths`: each row's source count and target count; positions at or past a count are padding.
All inputs are finite; a program needn't handle non-finite values.
Results may differ from a plain program's by a relative error of at most 0.017.
Values may be sent and summed in bfloat16 or wider, within the bound.
A program may use at most 128 MiB of HBM per device.

v0:
```python
import math

import jax
import jax.numpy as jnp
from jax import lax
from jax.sharding import PartitionSpec as P

HEAD = 128


EPS = 1e-06
MASKED = -1e30


def passed_along(shard, axis, by):
    peers = lax.axis_size(axis)
    pairs = [(i, i + by) for i in range(peers) if 0 <= i + by < peers]
    return lax.ppermute(shard, axis, pairs)


def contract_rows(left, right):
    return lax.dot_general(
        left, right, (((0,), (0,)), ((), ())), preferred_element_type=jnp.float32
    )


def contract_last(left, right):
    return lax.dot_general(
        left, right, (((1,), (1,)), ((), ())), preferred_element_type=jnp.float32
    )


def total_features(partial_value):
    return lax.psum(partial_value, "mp")


def split_heads(values_in):
    batch_size, length, columns = values_in.shape
    return values_in.reshape(batch_size, length, columns // HEAD, HEAD)


def attend(queries, keys, values, key_count):
    batch_size, length, columns = queries.shape
    scale = 1.0 / math.sqrt(HEAD)
    scores = (
        jnp.einsum(
            "bqhd,bkhd->bhqk",
            split_heads(queries),
            split_heads(keys),
            preferred_element_type=jnp.float32,
        )
        * scale
    )
    visible = jnp.arange(length)[None, None, None, :] < key_count[:, None, None, None]
    scores = jnp.where(visible, scores, MASKED)
    weights = jax.nn.softmax(scores, axis=-1)
    weights_low = weights.astype(jnp.bfloat16)
    context = jnp.einsum(
        "bhqk,bkhd->bqhd", weights_low, split_heads(values), preferred_element_type=jnp.float32
    )
    return (context.reshape(batch_size, length, columns).astype(jnp.bfloat16), weights, weights_low)


def attend_back(grad_context, queries, keys, values, weights, weights_low):
    batch_size, length, columns = queries.shape
    scale = 1.0 / math.sqrt(HEAD)
    grad_heads = split_heads(grad_context)
    grad_weights = jnp.einsum(
        "bqhd,bkhd->bhqk", grad_heads, split_heads(values), preferred_element_type=jnp.float32
    )
    grad_values = jnp.einsum(
        "bhqk,bqhd->bkhd", weights_low, grad_heads, preferred_element_type=jnp.float32
    )
    centered = grad_weights - jnp.sum(weights * grad_weights, axis=-1, keepdims=True)
    grad_scores = (weights * centered * scale).astype(jnp.bfloat16)
    grad_queries = jnp.einsum(
        "bhqk,bkhd->bqhd", grad_scores, split_heads(keys), preferred_element_type=jnp.float32
    )
    grad_keys = jnp.einsum(
        "bhqk,bqhd->bkhd", grad_scores, split_heads(queries), preferred_element_type=jnp.float32
    )
    shape_out = (batch_size, length, columns)
    return (
        grad_queries.reshape(shape_out).astype(jnp.bfloat16),
        grad_keys.reshape(shape_out).astype(jnp.bfloat16),
        grad_values.reshape(shape_out).astype(jnp.bfloat16),
    )


def shards(hidden, gain, w_first, w_second, lengths, cotangent):
    encoder = lax.axis_index("section") == 0
    states = hidden[0]
    batch_size, length, width = states.shape
    total_rows = batch_size * length
    gains = gain[0]
    wide = states.astype(jnp.float32)
    inverse = lax.rsqrt(jnp.mean(wide * wide, axis=-1, keepdims=True) + EPS)
    unit = wide * inverse
    normed = (unit * gains).astype(jnp.bfloat16)
    normed_rows = normed.reshape(total_rows, width)
    full_first, full_second = (
        lax.all_gather(w_first[0], "dp", axis=0, tiled=True),
        lax.all_gather(w_second[0], "dp", axis=0, tiled=True),
    )
    columns = full_first.shape[1]
    proj_shape = (batch_size, length, columns)
    first_proj = (
        jnp.dot(normed_rows, full_first, preferred_element_type=jnp.float32)
        .astype(jnp.bfloat16)
        .reshape(proj_shape)
    )

    def values_encoder(operand):
        return (
            jnp.dot(normed_rows, full_second, preferred_element_type=jnp.float32)
            .astype(jnp.bfloat16)
            .reshape(proj_shape)
        )

    def values_decoder(operand):
        return jnp.zeros(proj_shape, jnp.bfloat16)

    second_proj = lax.cond(encoder, values_encoder, values_decoder, 0)
    keys, values = passed_along((first_proj, second_proj), "section", 1)
    heads_here = columns // HEAD
    weight_shape = (batch_size, heads_here, length, length)

    def forward_decoder(operand):
        context, weights, weights_low = attend(first_proj, keys, values, lengths[:, 0])
        out_part = contract_last(context.reshape(total_rows, columns), full_second)
        return (context, weights, weights_low, out_part)

    def forward_encoder(operand):
        return (
            jnp.zeros(proj_shape, jnp.bfloat16),
            jnp.zeros(weight_shape, jnp.float32),
            jnp.zeros(weight_shape, jnp.bfloat16),
            jnp.zeros((total_rows, width), jnp.float32),
        )

    context, weights, weights_low, out_part = lax.cond(encoder, forward_encoder, forward_decoder, 0)
    wide_rows = wide.reshape(total_rows, width)
    unit_rows = unit.reshape(total_rows, width)
    inverse_rows = inverse.reshape(total_rows, 1)
    output_rows = (wide_rows + total_features(out_part)).astype(jnp.bfloat16)
    result = jnp.where(encoder, normed, output_rows.reshape(batch_size, length, width))
    target_keep = jnp.arange(length)[None, :] < lengths[:, 1][:, None]
    grad_out = jnp.where(target_keep[:, :, None], cotangent[0], jnp.zeros((), jnp.bfloat16))
    grad_out_rows = grad_out.reshape(total_rows, width)

    def backward_decoder(operand):
        grad_context = (
            jnp.dot(grad_out_rows, full_second, preferred_element_type=jnp.float32)
            .astype(jnp.bfloat16)
            .reshape(proj_shape)
        )
        return attend_back(grad_context, first_proj, keys, values, weights, weights_low)

    def backward_encoder(operand):
        empty = jnp.zeros(proj_shape, jnp.bfloat16)
        return (empty, empty, empty)

    grad_query, grad_key, grad_value = lax.cond(encoder, backward_encoder, backward_decoder, 0)
    back_key, back_value = passed_along((grad_key, grad_value), "section", -1)
    grad_first = jnp.where(encoder, back_key, grad_query).reshape(total_rows, columns)
    grad_second = jnp.where(encoder, back_value, jnp.zeros((), jnp.bfloat16)).reshape(
        total_rows, columns
    )
    second_left = jnp.where(encoder, normed, grad_out).reshape(total_rows, width)
    second_right = jnp.where(encoder, back_value, context).reshape(total_rows, columns)
    weight_first = contract_rows(normed_rows, grad_first)
    weight_second = contract_rows(second_left, second_right)

    def back_encoder(operand):
        return contract_last(grad_first, full_first) + contract_last(grad_second, full_second)

    def back_decoder(operand):
        return contract_last(grad_first, full_first)

    back_part = lax.cond(encoder, back_encoder, back_decoder, 0)
    extra_rows = jnp.where(encoder, cotangent[0].astype(jnp.float32), 0.0).reshape(
        total_rows, width
    )
    residual_rows = jnp.where(encoder, 0.0, grad_out.astype(jnp.float32)).reshape(total_rows, width)
    grad_normed = total_features(back_part) + extra_rows
    scaled = grad_normed * gains
    inner = jnp.mean(scaled * unit_rows, axis=-1, keepdims=True)
    grad_states = (inverse_rows * (scaled - unit_rows * inner) + residual_rows).astype(jnp.bfloat16)
    gain_part = jnp.sum(grad_normed * unit_rows, axis=0)
    first_sum, second_sum, gain_sum = (
        lax.psum_scatter(
            weight_first.astype(jnp.bfloat16), "dp", scatter_dimension=0, tiled=True
        ).astype(jnp.float32),
        lax.psum_scatter(
            weight_second.astype(jnp.bfloat16), "dp", scatter_dimension=0, tiled=True
        ).astype(jnp.float32),
        lax.psum_scatter(
            gain_part.astype(jnp.bfloat16), "dp", scatter_dimension=0, tiled=True
        ).astype(jnp.float32),
    )
    return (
        result[None],
        grad_states.reshape(batch_size, length, width)[None],
        gain_sum[None],
        first_sum[None],
        second_sum[None],
    )


def solution(mesh):
    return jax.shard_map(
        shards,
        mesh=mesh,
        in_specs=(
            P("section", "dp", None, None),
            P("section", None),
            P("section", "dp", "mp"),
            P("section", "dp", "mp"),
            P("dp", None),
            P("section", "dp", None, None),
        ),
        out_specs=(
            P("section", "dp", None, None),
            P("section", "dp", None, None),
            P("section", "dp"),
            P("section", "dp", "mp"),
            P("section", "dp", "mp"),
        ),
        check_vma=False,
    )
```

profile of v0, /device:TPU:2, one launch (start us, length us, event | category | flops | bytes accessed | tf_op | source)
XLA Modules:
  0.0 681.9 jit_solution(3879700864426107040)
XLA Ops:
  13.0 3.0 fusion.28
  16.0 61.1 %all-gather.5.cloned.1.call-done = bf16[1,5120,640]{2,1,0:T(8,128)(2,1)} async-done(((bf16[1,320,640]{2,1,0:T(8,128)(2,1)}), bf16[1,5120,640]{2,1,0:T(8,128)(2,1)}) %all-gather.5.cloned.1.call-update) | async-done | bytes 6553616 | tf_op jit(solution)/shard_map/all_gather | solution.py:102
  77.1 5.1 convolution_convert_fusion.8
  83.5 60.9 %all-gather.7.cloned.1.call-done = bf16[1,5120,640]{2,1,0:T(8,128)(2,1)} async-done(((bf16[1,320,640]{2,1,0:T(8,128)(2,1)}), bf16[1,5120,640]{2,1,0:T(8,128)(2,1)}) %all-gather.7.cloned.1.call-update) | async-done | bytes 6553616 | tf_op jit(solution)/shard_map/all_gather | solution.py:103
  146.7 3.5 bitcast_select_fusion
  150.2 12.2 %collective-permute-done.1 = bf16[1,256,640]{1,2,0:T(8,128)(2,1)} collective-permute-done((bf16[1,256,640]{1,2,0:T(8,128)(2,1)}, bf16[1,256,640]{1,2,0:T(8,128)(2,1)}, u32[]{:S(2)}, u32[]{:S(2)}) %collective-permute-start.1) | collective-permute-done | bytes 327712 | tf_op jit(solution)/shard_map/ppermute | solution.py:18
  162.4 13.9 %conditional.5 = (f32[1,5,256,256]{2,3,1,0:T(8,128)}, bf16[1,5,256,256]{2,3,1,0:T(8,128)(2,1)S(1)}, f32[256,5120]{1,0:T(8,128)}, bf16[1,256,640]{2,1,0:T(8,128)(2,1)}) conditional(s32[]{:T(128)} %convert_element_type.199, (s32[1,2]{1,0:T(1,128)S(1)}, bf16[256,640]{1,0:T(8,128)(2,1)S(1)}, bf16[1,256,640]{2,1,0:T(8,128)(2,1)}, ...), branch_computations={%region_3.6_spmd, %region_6.7_spmd} | conditional | flops 1848279552 | bytes 48840284 | solution.py:141
  165.4 2.7 fusion.10
  169.9 4.5 fusion.60
  176.3 23.3 %conditional.6 = (bf16[1,256,640]{1,2,0:T(8,128)(2,1)}, bf16[1,256,640]{1,2,0:T(8,128)(2,1)}, bf16[1,256,640]{2,1,0:T(8,128)(2,1)S(1)}) conditional(s32[]{:T(128)} %convert_element_type.199, (bf16[256,5120]{1,0:T(8,128)(2,1)}, bf16[5120,640]{1,0:T(8,128)(2,1)}, bf16[1,256,640]{1,2,0:T(8,128)(2,1)}, f32[1,5,256,256]{2,3,1,0:T(8,128)}, ...), branch_computations={%region_8.10_spmd, %region_10.11_spmd} | conditional | flops 2015886080 | bytes 26552400 | solution.py:163
  177.1 6.6 convolution_convert_fusion.5
  202.1 7.1 %collective-permute-done.2 = bf16[1,256,640]{2,1,0:T(8,128)(2,1)S(1)} collective-permute-done((bf16[1,256,640]{2,1,0:T(8,128)(2,1)S(1)}, bf16[1,256,640]{2,1,0:T(8,128)(2,1)S(1)}, u32[]{:S(2)}, u32[]{:S(2)}) %collective-permute-start.2) | collective-permute-done | bytes 327712 | tf_op jit(solution)/shard_map/ppermute | solution.py:18
  209.3 5.1 convolution_convert_fusion.7
  216.3 4.4 collective-permute-start.3
  220.7 6.6 collective-permute-done.3
  227.3 7.8 %convolution_convert_fusion.6 = bf16[5120,640]{1,0:T(8,128)(2,1)} fusion(bf16[1,1,256,5120]{3,2,1,0:T(8,128)(2,1)} %param.19, pred[256]{0:T(512)(128)(4,1)S(1)} %iota_compare_fusion.1, pred[]{:T(512)} %eq.3, bf16[1,1,256,5120]{3,2,1,0:T(8,128)(2,1)S(1)} %copy-done, f32[5120]{0:T(1024)S(1)} %bitcast.184, f32[256]{0:T(256)S(1)} %add_rsqrt_fusion, ...), kind=kOutput, calls=%fused_computation.33 | convolution fusion | flops 1689026560 | bytes 12473601 | tf_op jit(solution)/shard_map/dot_general | solution.py:22
  235.2 7.9 %conditional.7 = (f32[256,5120]{1,0:T(8,128)}) conditional(s32[]{:T(128)} %convert_element_type.199, (bf16[256,640]{1,0:T(8,128)(2,1)S(1)}, bf16[5120,640]{1,0:T(8,128)(2,1)}) %tuple.78, (bf16[256,640]{1,0:T(8,128)(2,1)S(1)}, bf16[5120,640]{1,0:T(8,128)(2,1)}, pred[]{:T(512)}, bf16[1,256,640]{2,1,0:T(8,128)(2,1)S(1)}, ...), branch_computations={%region_11.12_spmd, %region_12.13_spmd} | conditional | flops 3356917760 | bytes 55705636 | solution.py:180
  235.2 7.9 %fusion.58 = f32[256,5120]{1,0:T(8,128)} fusion(bf16[256,640]{1,0:T(8,128)(2,1)S(1)} %get-tuple-element.67, bf16[5120,640]{1,0:T(8,128)(2,1)} %get-tuple-element.68), kind=kOutput, calls=%fused_computation.81 | convolution fusion | flops 1677721600 | bytes 12124160 | tf_op jit(solution)/shard_map/cond/branch_0_fun/dot_general | solution.py:28
  245.0 58.7 %reduce-scatter.3.cloned.1.call-done = bf16[320,640]{1,0:T(8,128)(2,1)} async-done(((bf16[5120,640]{1,0:T(8,128)(2,1)}), bf16[320,640]{1,0:T(8,128)(2,1)}) %reduce-scatter.3.cloned.1.call-update) | async-done | bytes 409616 | tf_op jit(solution)/shard_map/reduce_scatter | solution.py:191
  305.6 92.4 %reduce-scatter.5.cloned.1.call-done = bf16[320,640]{1,0:T(8,128)(2,1)} async-done(((bf16[5120,640]{1,0:T(8,128)(2,1)}), bf16[320,640]{1,0:T(8,128)(2,1)}) %reduce-scatter.5.cloned.1.call-update) | async-done | bytes 409616 | tf_op jit(solution)/shard_map/reduce_scatter | solution.py:194
  399.9 195.0 %all-reduce.4.cloned.1.call-done = (f32[256,5120]{1,0:T(8,128)}, f32[256,5120]{1,0:T(8,128)}) async-done(((f32[256,5120]{1,0:T(8,128)}, f32[256,5120]{1,0:T(8,128)}), (f32[256,5120]{1,0:T(8,128)}, f32[256,5120]{1,0:T(8,128)})) %all-reduce.4.cloned.1.call-update) | async-done | bytes 10485776 | tf_op jit(solution)/shard_map/psum | solution.py:34
  594.9 5.3 fusion.40
  602.4 3.8 fusion.41
  606.3 68.5 %all-reduce = bf16[5120]{0:T(1024)(128)(2,1)S(1)} all-reduce(bf16[5120]{0:T(1024)(128)(2,1)S(1)} %get-tuple-element.131), channel_id=4, replica_groups=mesh['section'=2,'dp'=16,'mp'=4] {'dp'}, use_global_device_ids=true, to_apply=%region_16.17.clone | all-reduce | flops 5120 | bytes 20480
  (70 shorter events, 45.0 us)
Async XLA Ops:
  7.2 5.8 copy-start
  7.2 69.9 %copy-start.10 = (f32[1,5120]{1,0:T(1,128)S(1)}, f32[1,5120]{1,0:T(1,128)}, u32[]{:S(2)}) copy-start(f32[1,5120]{1,0:T(1,128)} %param.15) | copy-start | bytes 61444
  7.2 69.9 %all-gather.5.cloned.1.call-start = ((), (), s32[]{:S(2)}) async-start(), calls=%async_computation.4 | async-start | bytes 6963200 | tf_op jit(solution)/shard_map/all_gather | solution.py:102
  7.9 136.5 %all-gather.7.cloned.1.call-start = ((), (), s32[]{:S(2)}) async-start(), calls=%async_computation.5 | async-start | bytes 6963200 | tf_op jit(solution)/shard_map/all_gather | solution.py:103
  8.7 295.0 %reduce-scatter.3.cloned.1.call-start = ((), (), s32[]{:S(2)}) async-start(), calls=%async_computation.2 | async-start | bytes 6963200 | tf_op jit(solution)/shard_map/reduce_scatter | solution.py:191
  82.2 80.2 %copy-start.9 = (bf16[256,640]{1,0:T(8,128)(2,1)}, bf16[256,640]{1,0:T(8,128)(2,1)S(1)}, u32[]{:S(2)}) copy-start(bf16[256,640]{1,0:T(8,128)(2,1)S(1)} %convolution_convert_fusion.8) | copy-start | bytes 983044
  82.2 68.0 %collective-permute-start = (bf16[1,256,640]{2,1,0:T(8,128)(2,1)S(1)}, bf16[1,256,640]{2,1,0:T(8,128)(2,1)}, u32[]{:S(2)}, u32[]{:S(2)}) collective-permute-start(bf16[1,256,640]{2,1,0:T(8,128)(2,1)S(1)} %bitcast.180), channel_id=1, source_target_pairs={{0,64},{1,65},{2,66},{3,67},{4,68},{5,69},{6,70},{7,71},{8,72},{9,... | collective-permute-start | bytes 983048 | tf_op jit(solution)/shard_map/ppermute | solution.py:18
  144.5 17.9 %copy-start.11 = (s32[1,2]{1,0:T(1,128)S(1)}, s32[1,2]{1,0:T(1,128)}, u32[]{:S(2)}) copy-start(s32[1,2]{1,0:T(1,128)} %param.18) | copy-start | bytes 28
  145.4 17.0 %collective-permute-start.1 = (bf16[1,256,640]{1,2,0:T(8,128)(2,1)}, bf16[1,256,640]{1,2,0:T(8,128)(2,1)}, u32[]{:S(2)}, u32[]{:S(2)}) collective-permute-start(bf16[1,256,640]{1,2,0:T(8,128)(2,1)} %copy.53), channel_id=1, source_target_pairs={{0,64},{1,65},{2,66},{3,67},{4,68},{5,69},{6,70},{7,71},{8,72},{9,... | collective-permute-start | bytes 983048 | tf_op jit(solution)/shard_map/ppermute | solution.py:18
  165.4 4.4 copy-start.1
  169.8 4.6 copy-start.7
  176.3 0.8 copy-start.6
  184.9 1.9 copy-start.5
  200.8 8.5 %collective-permute-start.2 = (bf16[1,256,640]{2,1,0:T(8,128)(2,1)S(1)}, bf16[1,256,640]{2,1,0:T(8,128)(2,1)S(1)}, u32[]{:S(2)}, u32[]{:S(2)}) collective-permute-start(bf16[1,256,640]{2,1,0:T(8,128)(2,1)S(1)} %copy.59), channel_id=1, source_target_pairs={{64,0},{65,1},{66,2},{67,3},{68,4},{69,5},{70,6},{71,7},{72,8},{73... | collective-permute-start | bytes 983048 | tf_op jit(solution)/shard_map/ppermute | solution.py:18
  214.4 1.0 copy-start.8
  214.4 183.5 %reduce-scatter.5.cloned.1.call-start = ((), (), s32[]{:S(2)}) async-start(), calls=%async_computation.3 | async-start | bytes 6963200 | tf_op jit(solution)/shard_map/reduce_scatter | solution.py:194
  216.3 11.0 %collective-permute-start.3 = (bf16[1,256,640]{2,1,0:T(8,128)(2,1)}, bf16[1,256,640]{2,1,0:T(8,128)(2,1)S(1)}, u32[]{:S(2)}, u32[]{:S(2)}) collective-permute-start(bf16[1,256,640]{2,1,0:T(8,128)(2,1)} %copy.61), channel_id=1, source_target_pairs={{64,0},{65,1},{66,2},{67,3},{68,4},{69,5},{70,6},{71,7},{72,8},{73... | collective-permute-start | bytes 983048 | tf_op jit(solution)/shard_map/ppermute | solution.py:18
  235.1 359.8 %all-reduce.4.cloned.1.call-start = ((), (), s32[]{:S(2)}) async-start(), calls=%async_computation.6 | async-start | bytes 20971520 | tf_op jit(solution)/shard_map/psum | solution.py:34
  243.1 0.7 copy-start.12
  594.9 5.3 copy-start.3
  594.9 5.3 copy-start.4
Sparse Core Ops, SparseCore 0:
  10.5 66.5 all-gather.4
  79.5 64.8 all-gather.6
  214.5 89.0 reduce-scatter.2
  308.3 89.6 reduce-scatter.4
  400.4 194.4 all-reduce.3
where the time goes:
time: 684 us; the launch traced here: 682 us
  waiting for transfers between devices  495 us (72%)
  blocking collectives  68.5 us (10%)
  matrix products  48.7 us (7%)
  other arithmetic  29.1 us (4%)
  local copies, waits for them, and re-layouts  17 us (2%)
  between operations  14.6 us (2%)
  starting transfers between devices  8.47 us (1%)
    psum x1, waiting for transfers between devices, total_features(): return lax.psum(partial_value, 'mp')  195 us
    reduce_scatter x1, waiting for transfers between devices, shards(): lax.psum_scatter(weight_second.astype(jnp.bfloat16), 'dp', scatter_dimens...  92.4 us
    unnamed x1, blocking collectives  68.5 us
    all_gather x1, waiting for transfers between devices, shards(): lax.all_gather(w_first[0], 'dp', axis=0, tiled=True)  61.1 us
    all_gather x1, waiting for transfers between devices, shards(): lax.all_gather(w_second[0], 'dp', axis=0, tiled=True)  60.9 us
    reduce_scatter x1, waiting for transfers between devices, shards(): lax.psum_scatter(weight_first.astype(jnp.bfloat16), 'dp', scatter_dimensi...  58.7 us
    ppermute x4, waiting for transfers between devices, passed_along(): return lax.ppermute(shard, axis, pairs)  26 us
  transfers between devices with their start and end apart: 9, of which 8 were waited for; matrix products, arithmetic and copies ran while one was open for 6% of the time, Pallas kernels for 0%

commit v1 on v0

v1 whole, which is shorter than its diff:
```python
import functools
import math

import jax
import jax.numpy as jnp
from jax import lax
from jax.experimental import pallas as pl
from jax.experimental.pallas import tpu as pltpu
from jax.sharding import PartitionSpec as P

HEAD = 128
EPS = 1e-06
MASKED = -1e30
MESH = pl.DeviceIdType.MESH
BF = jnp.bfloat16
F32 = jnp.float32
NY = 4
NZ = 4
VMEM_LIMIT = 66_000_000


def spec(space):
    return pl.BlockSpec(memory_space=space)


def coords():
    d = lax.axis_index("dp")
    return d // (2 * NY), (d // 2) % NY, d % 2


def dp_of(xh, y, c):
    return (xh * NY + y) * 2 + c


def greet(peers):
    barrier = pltpu.get_barrier_semaphore()
    for peer in peers:
        pl.semaphore_signal(barrier, inc=1, device_id=peer, device_id_type=MESH)
    pl.semaphore_wait(barrier, len(peers))


def remote(src, dst, ssem, rsem, peer):
    return pltpu.make_async_remote_copy(
        src_ref=src, dst_ref=dst, send_sem=ssem, recv_sem=rsem, device_id=peer, device_id_type=MESH
    )


def gather_kernel(
    len_ref, hid_in, cot_in, gain_ref, wf_in, ws_in,
    wfull_out, act_out, proj_ref,
    w, hid, act, acc, ssem, rsem, lsem, osem,
):
    sec = lax.axis_index("section")
    xh, y, c = coords()
    oh = 1 - xh
    yp, ym, yf = (y + 1) % NY, (y + 3) % NY, (y + 2) % NY
    half = w.shape[3] // 2
    length, width = hid.shape
    pair = 2 * w.shape[3]
    sources = (wf_in, ws_in)

    partner = {"dp": dp_of(xh, y, 1 - c)}
    xpeer = {"dp": dp_of(oh, y, c)}
    up = {"dp": dp_of(xh, yp, c)}
    down = {"dp": dp_of(xh, ym, c)}

    low, high = pl.ds(0, half), pl.ds(half, half)
    kinds = (
        ((xh, y), None, xpeer),
        ((xh, y), None, up),
        ((xh, y), None, down),
        ((oh, y), None, up),
        ((oh, y), None, down),
        ((xh, ym), low, up),
        ((xh, yp), high, down),
        ((oh, ym), low, up),
        ((oh, yp), high, down),
        ((xh, y), None, partner),
        ((oh, y), None, partner),
        ((xh, ym), None, partner),
        ((xh, yp), None, partner),
        ((oh, ym), None, partner),
        ((oh, yp), None, partner),
        ((xh, yf), None, partner),
        ((oh, yf), None, partner),
    )
    own = (0, 1, 2, 9)

    def message(t, k):
        (h, yy), rows, peer = kinds[k]
        place = w.at[t, h * NY + yy, c]
        if rows is not None:
            place = w.at[t, h * NY + yy, c, rows]
        src = sources[t] if k in own else place
        return remote(src, place, ssem.at[t, k], rsem.at[t, k], peer)

    def start(t, *ks):
        for k in ks:
            message(t, k).start()

    def arrived(t, *ks):
        for k in ks:
            message(t, k).wait_recv()

    hid_copy = pltpu.make_async_copy(hid_in, hid, lsem.at[0])
    cot_copy = pltpu.make_async_copy(cot_in, act.at[1], lsem.at[1])
    own_copy = [
        pltpu.make_async_copy(sources[t], w.at[t, xh * NY + y, c], lsem.at[2 + t]) for t in range(2)
    ]
    hid_copy.start()
    cot_copy.start()
    for copy in own_copy:
        copy.start()
    greet([partner, xpeer, up, down])
    start(0, 0, 1, 2, 9)
    start(1, 0, 9)

    hid_copy.wait()
    cot_copy.wait()
    target_count = len_ref[0, 1]
    block = 16

    def norm_rows(i, carry):
        rows = pl.ds(pl.multiple_of(i * block, block), block)
        wide = hid[rows, :].astype(F32)
        inverse = lax.rsqrt(jnp.mean(wide * wide, axis=-1, keepdims=True) + EPS)
        act[0, rows, :] = (wide * inverse * gain_ref[...]).astype(BF)
        row = i * block + lax.broadcasted_iota(jnp.int32, (block, 1), 0)
        keep = jnp.logical_or(row < target_count, sec == 0)
        act[1, rows, :] = jnp.where(keep, act[1, rows, :].astype(F32), 0.0).astype(BF)
        return carry

    lax.fori_loop(0, length // block, norm_rows, 0)
    for copy in own_copy:
        copy.wait()

    saved = []

    def use(t, h, yy, first=False):
        p = h * NY + yy
        columns = pl.ds(pl.multiple_of(p * pair, 128), pair)
        copy = pltpu.make_async_copy(w.at[t, p], wfull_out.at[t, p], osem.at[len(saved)])
        copy.start()
        saved.append(copy)
        left = act[0, :, columns] if t == 0 else act[sec, :, columns]
        part = jnp.dot(left, w[t, p].reshape(pair, w.shape[4]), preferred_element_type=F32)
        if first:
            acc[t] = part
        else:
            acc[t] += part

    act_copy = pltpu.make_async_copy(act, act_out, lsem.at[4])
    act_copy.start()

    arrived(0, 1)
    start(0, 5, 11)
    arrived(0, 2)
    start(0, 6, 12)
    start(1, 1, 2)
    arrived(0, 9)
    use(0, xh, y, True)
    arrived(1, 9)
    use(1, xh, y, True)
    arrived(0, 0)
    start(0, 3, 4, 10)
    arrived(0, 11)
    use(0, xh, ym)
    arrived(0, 12)
    use(0, xh, yp)
    arrived(0, 5, 6)
    start(0, 15)
    arrived(0, 10)
    use(0, oh, y)
    arrived(1, 1)
    start(1, 5, 11)
    arrived(1, 2)
    start(1, 6, 12)
    arrived(0, 15)
    use(0, xh, yf)
    arrived(1, 0)
    start(1, 3, 4, 10)
    arrived(0, 3)
    start(0, 7, 13)
    arrived(0, 4)
    start(0, 8, 14)
    arrived(1, 11)
    use(1, xh, ym)
    arrived(1, 12)
    use(1, xh, yp)
    arrived(0, 13)
    use(0, oh, ym)
    arrived(0, 14)
    use(0, oh, yp)
    arrived(0, 7, 8)
    start(0, 16)
    arrived(1, 10)
    use(1, oh, y)
    arrived(1, 5, 6)
    start(1, 15)
    arrived(0, 16)
    use(0, oh, yf)
    proj_ref[0] = acc[0].astype(BF)
    arrived(1, 15)
    use(1, xh, yf)
    arrived(1, 3)
    start(1, 7, 13)
    arrived(1, 4)
    start(1, 8, 14)
    arrived(1, 13)
    use(1, oh, ym)
    arrived(1, 14)
    use(1, oh, yp)
    arrived(1, 7, 8)
    start(1, 16)
    arrived(1, 16)
    use(1, oh, yf)
    proj_ref[1] = acc[1].astype(BF)

    for t in range(2):
        for k in range(len(kinds)):
            message(t, k).wait_send()
    act_copy.wait()
    for copy in saved:
        copy.wait()


def gather_call(lengths, hidden, cotangent, gain, w_first, w_second):
    length, width = hidden.shape
    depth, columns = w_first.shape
    return pl.pallas_call(
        gather_kernel,
        out_shape=(
            jax.ShapeDtypeStruct((2, 2 * NY, 2, depth, columns), BF),
            jax.ShapeDtypeStruct((2, length, width), BF),
            jax.ShapeDtypeStruct((2, length, columns), BF),
        ),
        in_specs=[
            spec(pltpu.SMEM), spec(pl.ANY), spec(pl.ANY), spec(pltpu.VMEM), spec(pl.ANY), spec(pl.ANY),
        ],
        out_specs=(spec(pl.ANY), spec(pl.ANY), spec(pltpu.VMEM)),
        scratch_shapes=[
            pltpu.VMEM((2, 2 * NY, 2, depth, columns), BF),
            pltpu.VMEM((length, width), BF),
            pltpu.VMEM((2, length, width), BF),
            pltpu.VMEM((2, length, columns), F32),
            pltpu.SemaphoreType.DMA((2, 17)),
            pltpu.SemaphoreType.DMA((2, 17)),
            pltpu.SemaphoreType.DMA((5,)),
            pltpu.SemaphoreType.DMA((16,)),
        ],
        compiler_params=pltpu.CompilerParams(
            collective_id=0, has_side_effects=True, vmem_limit_bytes=VMEM_LIMIT
        ),
        name="gather_project",
    )(lengths, hidden, cotangent, gain, w_first, w_second)


def attend_kernel(len_ref, proj, out_ref, got, give, ssem, rsem):
    sec = lax.axis_index("section")
    other = {"section": 1 - sec}
    heads = proj.shape[2] // HEAD
    length = proj.shape[1]
    scale = 1.0 / math.sqrt(HEAD)
    greet([other])

    def columns(h):
        return pl.ds(h * HEAD, HEAD)

    def forward(h, i):
        return remote(
            proj.at[i, :, columns(h)], got.at[i, :, columns(h)], ssem.at[i, h], rsem.at[i, h], other
        )

    def backward(h, i):
        return remote(
            give.at[i, :, columns(h)], got.at[i, :, columns(h)], ssem.at[i, h], rsem.at[i, h], other
        )

    def nt(a, b):
        return lax.dot_general(a, b, (((1,), (1,)), ((), ())), preferred_element_type=F32)

    def tn(a, b):
        return lax.dot_general(a, b, (((0,), (0,)), ((), ())), preferred_element_type=F32)

    @pl.when(sec == 0)
    def _():
        for h in range(heads):
            forward(h, 0).start()
            forward(h, 1).start()
        for h in range(heads):
            for i in range(2):
                backward(h, i).wait_recv()
                out_ref[i, :, columns(h)] = got[i, :, columns(h)]
        for h in range(heads):
            for i in range(2):
                forward(h, i).wait_send()

    @pl.when(sec == 1)
    def _():
        visible = lax.broadcasted_iota(jnp.int32, (1, length), 1) < len_ref[0, 0]
        for h in range(heads):
            forward(h, 0).wait_recv()
            forward(h, 1).wait_recv()
            q = proj[0, :, columns(h)]
            gc = proj[1, :, columns(h)]
            k = got[0, :, columns(h)]
            v = got[1, :, columns(h)]
            scores = jnp.where(visible, nt(q, k) * scale, MASKED)
            top = jnp.max(scores, axis=-1, keepdims=True)
            e = jnp.exp(scores - top)
            weights = e / jnp.sum(e, axis=-1, keepdims=True)
            low = weights.astype(BF)
            grad_weights = nt(gc, v)
            inner = jnp.sum(weights * grad_weights, axis=-1, keepdims=True)
            grad_scores = (weights * (grad_weights - inner) * scale).astype(BF)
            give[0, :, columns(h)] = tn(grad_scores, q).astype(BF)
            give[1, :, columns(h)] = tn(low, gc).astype(BF)
            backward(h, 0).start()
            backward(h, 1).start()
            out_ref[0, :, columns(h)] = jnp.dot(grad_scores, k, preferred_element_type=F32).astype(BF)
            out_ref[1, :, columns(h)] = jnp.dot(low, v, preferred_element_type=F32).astype(BF)
        for h in range(heads):
            for i in range(2):
                backward(h, i).wait_send()


def attend_call(lengths, proj):
    heads = proj.shape[2] // HEAD
    return pl.pallas_call(
        attend_kernel,
        out_shape=jax.ShapeDtypeStruct(proj.shape, BF),
        in_specs=[spec(pltpu.SMEM), spec(pltpu.VMEM)],
        out_specs=spec(pltpu.VMEM),
        scratch_shapes=[
            pltpu.VMEM(proj.shape, BF),
            pltpu.VMEM(proj.shape, BF),
            pltpu.SemaphoreType.DMA((2, heads)),
            pltpu.SemaphoreType.DMA((2, heads)),
        ],
        compiler_params=pltpu.CompilerParams(collective_id=1, has_side_effects=True),
        name="attend_both",
    )(lengths, proj)


def reduce_kernel(
    hid_in, gain_ref, act_in, w_in, g,
    dw_ref, rows_out, gain_out,
    act, w, dwb, rp, rf, rn, xs, xr, zp, zf, zn, zo, hid, gz, gs,
    psem, prsem, fsem, frsem, nsem, nrsem, xsem, xrsem, zsem, zrsem, gsem, grsem, lsem,
):
    sec = lax.axis_index("section")
    z = lax.axis_index("mp")
    xh, y, c = coords()
    oh = 1 - xh
    yp, ym, yf = (y + 1) % NY, (y + 3) % NY, (y + 2) % NY
    zup, zdn, zfar = (z + 1) % NZ, (z + 3) % NZ, (z + 2) % NZ
    depth, columns = rp.shape[2:]
    half = depth // 2
    pair = 2 * depth
    length, width = act.shape[1:]
    rows = length // NZ
    hrows = rows // 2

    partner = {"dp": dp_of(xh, y, 1 - c)}
    xpeer = {"dp": dp_of(oh, y, c)}
    up = {"dp": dp_of(xh, yp, c)}
    down = {"dp": dp_of(xh, ym, c)}
    yfar = {"dp": dp_of(xh, yf, c)}
    above = {"mp": zup}
    below = {"mp": zdn}
    zopp = {"mp": zfar}

    act_copy = pltpu.make_async_copy(act_in, act, lsem.at[0])
    w_copy = pltpu.make_async_copy(w_in, w, lsem.at[1])
    hid_copy = pltpu.make_async_copy(
        hid_in.at[pl.ds(pl.multiple_of(z * rows, rows), rows)], hid, lsem.at[2]
    )
    act_copy.start()
    w_copy.start()
    hid_copy.start()
    greet([partner, xpeer, up, down, yfar, above, below, zopp])
    act_copy.wait()

    def to_partner(t, p):
        return remote(dwb.at[t, p, 1 - c], rp.at[t, p], psem.at[t, p], prsem.at[t, p], partner)

    def far_message(t, h, way):
        hh = oh if h == 0 else xh
        part = pl.ds(way * half, half)
        return remote(
            rp.at[t, hh * NY + yf, part], rf.at[t, h, way], fsem.at[t, h, way], frsem.at[t, h, way],
            up if way == 0 else down,
        )

    def near_message(t, h, way):
        hh = oh if h == 0 else xh
        return remote(
            rp.at[t, hh * NY + (yp if way == 0 else ym)], rn.at[t, h, way],
            nsem.at[t, h, way], nrsem.at[t, h, way], up if way == 0 else down,
        )

    def x_message(t):
        return remote(xs.at[t], xr.at[t], xsem.at[t], xrsem.at[t], xpeer)

    def products(hh, first, last):
        def body(j, carry):
            t = 1 - j % 2
            p = hh * NY + (y + 2 + j // 2) % NY
            left = act[t * sec, :, pl.ds(pl.multiple_of(p * pair, 128), pair)]
            out = lax.dot_general(left, g[t], (((0,), (0,)), ((), ())), preferred_element_type=F32)
            dwb[t, p] = out.astype(BF).reshape(2, depth, columns)
            to_partner(t, p).start()
            return carry

        lax.fori_loop(first, last, body, 0)

    def pair_sum(t, p, part=None):
        if part is None:
            part = pl.ds(0, depth)
        return dwb[t, p, c, part].astype(F32) + rp[t, p, part].astype(F32)

    def send_far(t, h):
        hh = oh if h == 0 else xh
        p = hh * NY + yf
        to_partner(t, p).wait_recv()
        rp[t, p] = pair_sum(t, p).astype(BF)
        far_message(t, h, 0).start()
        far_message(t, h, 1).start()

    def send_near(t, h):
        hh = oh if h == 0 else xh
        for way, yy in ((0, yp), (1, ym)):
            p = hh * NY + yy
            to_partner(t, p).wait_recv()
            far_message(t, h, way).wait_recv()
            mine, rest = pl.ds(way * half, half), pl.ds((1 - way) * half, half)
            rp[t, p, mine] = (pair_sum(t, p, mine) + rf[t, h, way].astype(F32)).astype(BF)
            rp[t, p, rest] = pair_sum(t, p, rest).astype(BF)
            near_message(t, h, way).start()

    def ring_total(t, h):
        hh = oh if h == 0 else xh
        p = hh * NY + y
        to_partner(t, p).wait_recv()
        near_message(t, h, 0).wait_recv()
        near_message(t, h, 1).wait_recv()
        return pair_sum(t, p) + rn[t, h, 0].astype(F32) + rn[t, h, 1].astype(F32)

    def z_rows(who, part=None):
        if part is None:
            return pl.ds(pl.multiple_of(who * rows, rows), rows)
        return pl.ds(pl.multiple_of(who * rows + part * hrows, hrows), hrows)

    def z_far(a, way):
        return remote(
            zp.at[a, z_rows(zfar, way)], zf.at[a, way], zsem.at[a, way], zrsem.at[a, way],
            above if way == 0 else below,
        )

    def z_near(a, way):
        return remote(
            zp.at[a, z_rows(zup if way == 0 else zdn)], zn.at[a, way], zsem.at[a, 2 + way],
            zrsem.at[a, 2 + way], above if way == 0 else below,
        )

    def z_own(a, way):
        place = zo.at[a, z_rows(z)]
        return remote(
            place, place, zsem.at[a, 4 + way], zrsem.at[a, 4 + way], above if way == 0 else below
        )

    def z_pass(a, way):
        place = zo.at[a, z_rows(zdn if way == 0 else zup, way)]
        return remote(
            place, place, zsem.at[a, 6 + way], zrsem.at[a, 6 + way], above if way == 0 else below
        )

    def head_product(a, terms):
        def body(p, carry):
            total = None
            for t in terms:
                right = w[t, p].reshape(pair, columns)
                part = lax.dot_general(g[t], right, (((1,), (1,)), ((), ())), preferred_element_type=F32)
                total = part if total is None else total + part
            zp[a, :, pl.ds(pl.multiple_of(p * pair, 128), pair)] = total.astype(BF)
            return carry

        lax.fori_loop(0, 2 * NY, body, 0)

    def z_send_near(a):
        for way, who in ((0, zup), (1, zdn)):
            z_far(a, way).wait_recv()
            place = z_rows(who, way)
            zp[a, place] = (zp[a, place].astype(F32) + zf[a, way].astype(F32)).astype(BF)
            z_near(a, way).start()

    def z_total(a, r, n):
        return (
            zp[a, pl.ds(pl.multiple_of(z * rows + r, n), n)].astype(F32)
            + zn[a, 0, pl.ds(r, n)].astype(F32)
            + zn[a, 1, pl.ds(r, n)].astype(F32)
        )

    def z_forward(a):
        for way in range(2):
            z_own(a, way).wait_recv()
            z_pass(a, way).start()

    block = 16

    def finish_output():
        z_near(0, 0).wait_recv()
        z_near(0, 1).wait_recv()

        def body(i, carry):
            r = pl.multiple_of(i * block, block)
            total = z_total(0, r, block) + hid[pl.ds(r, block)].astype(F32)
            zo[0, pl.ds(pl.multiple_of(z * rows + r, block), block)] = total.astype(BF)
            return carry

        lax.fori_loop(0, rows // block, body, 0)
        z_own(0, 0).start()
        z_own(0, 1).start()

    def finish_states():
        z_near(1, 0).wait_recv()
        z_near(1, 1).wait_recv()
        gains = gain_ref[...]

        def body(i, carry):
            r = pl.multiple_of(i * block, block)
            mine = pl.ds(pl.multiple_of(z * rows + r, block), block)
            wide = hid[pl.ds(r, block)].astype(F32)
            inverse = lax.rsqrt(jnp.mean(wide * wide, axis=-1, keepdims=True) + EPS)
            unit = wide * inverse
            extra = act[1, mine].astype(F32)
            grad = z_total(1, r, block) + jnp.where(sec == 0, extra, 0.0)
            scaled = grad * gains
            inner = jnp.mean(scaled * unit, axis=-1, keepdims=True)
            states = inverse * (scaled - unit * inner) + jnp.where(sec == 0, 0.0, extra)
            zo[1, mine] = states.astype(BF)
            gs[pl.ds(0, 1)] += jnp.sum(grad * unit, axis=0, keepdims=True)
            return carry

        gs[pl.ds(0, 1)] = jnp.zeros((1, width), F32)
        lax.fori_loop(0, rows // block, body, 0)
        for i in range(3):
            gain_z(i).start()
        z_own(1, 0).start()
        z_own(1, 1).start()

    gain_peers = (above, below, zopp, partner, xpeer, up, down, yfar)
    row0 = pl.ds(0, 1)

    def gain_z(i):
        return remote(gs.at[row0], gz.at[pl.ds(i, 1)], gsem.at[i], grsem.at[i], gain_peers[i])

    def gain_next(i, level):
        return remote(
            gs.at[pl.ds(level, 1)], gz.at[pl.ds(i, 1)], gsem.at[i], grsem.at[i], gain_peers[i]
        )

    products(oh, 0, 2)

    @pl.when(sec == 1)
    def _():
        w_copy.wait()
        head_product(0, (1,))
        z_far(0, 0).start()
        z_far(0, 1).start()

    send_far(1, 0)
    send_far(0, 0)
    products(oh, 2, 8)

    @pl.when(sec == 1)
    def _():
        head_product(1, (0,))
        z_send_near(0)

    @pl.when(sec == 0)
    def _():
        w_copy.wait()
        head_product(1, (0, 1))

    z_far(1, 0).start()
    z_far(1, 1).start()
    send_near(1, 0)
    send_near(0, 0)
    products(xh, 0, 2)
    send_far(1, 1)
    send_far(0, 1)
    products(xh, 2, 8)
    hid_copy.wait()

    @pl.when(sec == 1)
    def _():
        finish_output()

    z_send_near(1)
    for t in (1, 0):
        xs[t] = ring_total(t, 0).astype(BF)
        x_message(t).start()
    send_near(1, 1)
    send_near(0, 1)

    @pl.when(sec == 1)
    def _():
        z_forward(0)

    finish_states()
    z_forward(1)
    for i in range(3):
        gain_z(i).wait_recv()
    gs[pl.ds(1, 1)] = gs[row0] + gz[pl.ds(0, 1)] + gz[pl.ds(1, 1)] + gz[pl.ds(2, 1)]
    gain_next(3, 1).start()
    for t in (1, 0):
        total = ring_total(t, 1)
        x_message(t).wait_recv()
        dw_ref[t] = total + xr[t].astype(F32)
        if t == 1:
            gain_next(3, 1).wait_recv()
            gs[pl.ds(2, 1)] = gs[pl.ds(1, 1)] + gz[pl.ds(3, 1)]
            gain_next(4, 2).start()
    gain_next(4, 2).wait_recv()
    gs[pl.ds(3, 1)] = gs[pl.ds(2, 1)] + gz[pl.ds(4, 1)]
    for i in (5, 6, 7):
        gain_next(i, 3).start()
    for i in (5, 6, 7):
        gain_next(i, 3).wait_recv()
    gain_out[...] = gs[pl.ds(3, 1)] + gz[pl.ds(5, 1)] + gz[pl.ds(6, 1)] + gz[pl.ds(7, 1)]

    @pl.when(sec == 1)
    def _():
        z_pass(0, 0).wait_recv()
        z_pass(0, 1).wait_recv()
        out = pltpu.make_async_copy(zo.at[0], rows_out.at[0], lsem.at[3])
        out.start()
        out.wait()
        for way in range(2):
            for make in (z_far, z_near, z_own, z_pass):
                make(0, way).wait_send()

    @pl.when(sec == 0)
    def _():
        out = pltpu.make_async_copy(act.at[0], rows_out.at[0], lsem.at[3])
        out.start()
        out.wait()

    z_pass(1, 0).wait_recv()
    z_pass(1, 1).wait_recv()
    out = pltpu.make_async_copy(zo.at[1], rows_out.at[1], lsem.at[4])
    out.start()
    out.wait()
    for way in range(2):
        for make in (z_far, z_near, z_own, z_pass):
            make(1, way).wait_send()
    for i in range(3):
        gain_z(i).wait_send()
    for i, level in ((3, 1), (4, 2), (5, 3), (6, 3), (7, 3)):
        gain_next(i, level).wait_send()
    for t in range(2):
        x_message(t).wait_send()
        for h in range(2):
            for way in range(2):
                far_message(t, h, way).wait_send()
                near_message(t, h, way).wait_send()

    def drain(j, carry):
        to_partner(j % 2, j // 2).wait_send()
        return carry

    lax.fori_loop(0, 4 * NY, drain, 0)


def reduce_call(hidden, gain, act, w_full, g):
    length, width = hidden.shape
    depth, columns = w_full.shape[3:]
    rows = length // NZ
    dma = pltpu.SemaphoreType.DMA
    return pl.pallas_call(
        reduce_kernel,
        out_shape=(
            jax.ShapeDtypeStruct((2, depth, columns), F32),
            jax.ShapeDtypeStruct((2, length, width), BF),
            jax.ShapeDtypeStruct((1, width), F32),
        ),
        in_specs=[spec(pl.ANY), spec(pltpu.VMEM), spec(pl.ANY), spec(pl.ANY), spec(pltpu.VMEM)],
        out_specs=(spec(pltpu.VMEM), spec(pl.ANY), spec(pltpu.VMEM)),
        scratch_shapes=[
            pltpu.VMEM(act.shape, BF),
            pltpu.VMEM(w_full.shape, BF),
            pltpu.VMEM(w_full.shape, BF),
            pltpu.VMEM((2, 2 * NY, depth, columns), BF),
            pltpu.VMEM((2, 2, 2, depth // 2, columns), BF),
            pltpu.VMEM((2, 2, 2, depth, columns), BF),
            pltpu.VMEM((2, depth, columns), BF),
            pltpu.VMEM((2, depth, columns), BF),
            pltpu.VMEM((2, length, width), BF),
            pltpu.VMEM((2, 2, rows // 2, width), BF),
            pltpu.VMEM((2, 2, rows, width), BF),
            pltpu.VMEM((2, length, width), BF),
            pltpu.VMEM((rows, width), BF),
            pltpu.VMEM((8, width), F32),
            pltpu.VMEM((8, width), F32),
            dma((2, 2 * NY)), dma((2, 2 * NY)),
            dma((2, 2, 2)), dma((2, 2, 2)),
            dma((2, 2, 2)), dma((2, 2, 2)),
            dma((2,)), dma((2,)),
            dma((2, 8)), dma((2, 8)),
            dma((8,)), dma((8,)),
            dma((5,)),
        ],
        compiler_params=pltpu.CompilerParams(
            collective_id=2, has_side_effects=True, vmem_limit_bytes=VMEM_LIMIT
        ),
        name="reduce_all",
    )(hidden, gain, act, w_full, g)


def shards(hidden, gain, w_first, w_second, lengths, cotangent):
    states = hidden[0, 0]
    w_full, act, proj = gather_call(
        lengths, states, cotangent[0, 0], gain, w_first[0], w_second[0]
    )
    g = attend_call(lengths, proj)
    dw, rows, gain_sum = reduce_call(states, gain, act, w_full, g)
    depth = w_first.shape[1]
    gain_part = lax.dynamic_slice(gain_sum, (0, lax.axis_index("dp") * depth), (1, depth))
    return (rows[0][None, None], rows[1][None, None], gain_part, dw[0][None], dw[1][None])


def solution(mesh):
    return jax.shard_map(
        shards,
        mesh=mesh,
        in_specs=(
            P("section", "dp", None, None),
            P("section", None),
            P("section", "dp", "mp"),
            P("section", "dp", "mp"),
            P("dp", None),
            P("section", "dp", None, None),
        ),
        out_specs=(
            P("section", "dp", None, None),
            P("section", "dp", None, None),
            P("section", "dp"),
            P("section", "dp", "mp"),
            P("section", "dp", "mp"),
        ),
        check_vma=False,
    )
```

time: 684 us -> 207 us (0.30)
  waiting for transfers between devices: 495 us -> 0 us
  Pallas kernels: 0 us -> 198 us
  blocking collectives: 68.5 us -> 0 us
  matrix products: 48.7 us -> 0 us
  other arithmetic: 29.1 us -> 0 us
  between operations: 14.6 us -> 0.66 us
  local copies, waits for them, and re-layouts: 17 us -> 7.91 us
  starting transfers between devices: 8.47 us -> 0 us
    pallas_call x0 -> x3, Pallas kernels: none -> 198 us  [the longest x1 106 us: reduce_call(): pl.pallas_call(reduce_kernel, out_shape=(jax.ShapeDtypeStruct((2, depth,...]
    psum x1 -> x0, waiting for transfers between devices: 195 us -> none  [total_features(): return lax.psum(partial_value, 'mp')]
    reduce_scatter x2 -> x0, waiting for transfers between devices: 151 us -> none  [the longest x1 92.4 us: shards(): lax.psum_scatter(weight_second.astype(jnp.bfloat16), 'dp', scatter_dimens...]
    all_gather x2 -> x0, waiting for transfers between devices: 122 us -> none  [the longest x1 61.1 us: shards(): lax.all_gather(w_first[0], 'dp', axis=0, tiled=True)]
    unnamed x1 -> x0, blocking collectives: 68.5 us -> none
    dot_general x11 -> x0, matrix products: 47.1 us -> none  [the longest x2 12.9 us: contract_rows(): lax.dot_general(left, right, (((0,), (0,)), ((), ())), preferred_element_...]
    ppermute x4 -> x0, waiting for transfers between devices: 26 us -> none  [passed_along(): return lax.ppermute(shard, axis, pairs)]
    broadcast_in_dim x4 -> x0, other arithmetic: 9.24 us -> none  [the longest x1 5.28 us: shards(): result[None]]
  transfers between devices with their start and end apart: 9 -> 0, of which waited for: 8 -> 0; matrix products, arithmetic and copies ran while one was open for 6% -> 0% of each run, Pallas kernels for 0% -> 0%
where the time goes in v1:
time: 207 us
  Pallas kernels  198 us (96%)
  local copies, waits for them, and re-layouts  7.91 us (4%)
    pallas_call x1, Pallas kernels, reduce_call(): pl.pallas_call(reduce_kernel, out_shape=(jax.ShapeDtypeStruct((2, depth,...  106 us
    pallas_call x1, Pallas kernels, gather_call(): pl.pallas_call(gather_kernel, out_shape=(jax.ShapeDtypeStruct((2, 2 * NY,...  68.9 us
    pallas_call x1, Pallas kernels, attend_call(): pl.pallas_call(attend_kernel, out_shape=jax.ShapeDtypeStruct(proj.shape,...  23.1 us
    another operation x1, local copies, waits for them, and re-layouts, shards(): rows[1][None, None]  5.34 us

profile of v1, /device:TPU:2, one launch (start us, length us, event | category | flops | bytes accessed | tf_op | source)
XLA Modules:
  0.0 207.0 jit_solution(2868133767498258821)
XLA Ops:
  0.6 68.9 %gather_project.1 = (bf16[2,8,2,320,640]{4,3,2,1,0:T(8,128)(2,1)}, bf16[2,256,5120]{2,1,0:T(8,128)(2,1)}, bf16[2,256,640]{2,1,0:T(8,128)(2,1)}) custom-call(s32[1,2]{1,0:T(1,128)} %len_ref.3, bf16[256,5120]{1,0:T(8,128)(2,1)} %bitcast.8, bf16[256,5120]{1,0:T(8,128)(2,1)} %bitcast.10, f32[1,5120]{1,0:T(1,128)} %gain_ref.3, bf16[320,640]{1,0:T(8,128)(2,1)} %bitcast.11, ...), custom_call_target="tpu_custom_call" | custom-call | tf_op jit(solution)/shard_map/gather_project/pallas_call | solution.py:230
  69.5 23.1 %attend_both.1.g = bf16[2,256,640]{2,1,0:T(8,128)(2,1)} custom-call(s32[1,2]{1,0:T(1,128)} %len_ref.3, bf16[2,256,640]{2,1,0:T(8,128)(2,1)} %get-tuple-element.13.proj), custom_call_target="tpu_custom_call" | custom-call | tf_op jit(solution)/shard_map/attend_both/pallas_call | solution.py:329
  92.6 106.5 %reduce_all.1 = (f32[2,320,640]{2,1,0:T(8,128)}, bf16[2,256,5120]{2,1,0:T(8,128)(2,1)}, f32[1,5120]{1,0:T(1,128)}) custom-call(bf16[256,5120]{1,0:T(8,128)(2,1)} %bitcast.9, f32[1,5120]{1,0:T(1,128)} %gain_ref.3, bf16[2,256,5120]{2,1,0:T(8,128)(2,1)} %get-tuple-element.11.act_in, bf16[2,8,2,320,640]{4,3,2,1,0:T(8,128)(2,1)} %get-tuple-element.12.w_in, ...), custom_call_target="tpu_custom_call" | custom-call | tf_op jit(solution)/shard_map/reduce_all/pallas_call | solution.py:681
  199.1 1.3 constant_dynamic-slice_fusion
  200.4 0.0 copy-start
  200.4 5.3 %slice_bitcast_fusion = (bf16[1,1,256,5120]{3,2,1,0:T(8,128)(2,1)}, bf16[1,1,256,5120]{3,2,1,0:T(8,128)(2,1)}) fusion(bf16[2,256,5120]{2,1,0:T(8,128)(2,1)} %get-tuple-element.14), kind=kLoop, calls=%fused_computation | loop fusion | bytes 10485760 | tf_op jit(solution)/shard_map/broadcast_in_dim;squeeze | solution.py:730
  205.7 0.0 copy-done
  205.7 1.3 fusion
Async XLA Ops:
  200.4 5.3 %copy-start = (f32[2,320,640]{2,1,0:T(8,128)S(1)}, f32[2,320,640]{2,1,0:T(8,128)}, u32[]{:S(2)}) copy-start(f32[2,320,640]{2,1,0:T(8,128)} %get-tuple-element.16) | copy-start | bytes 4915204

commit v2 on v0

v2 whole, which is shorter than its diff:
```python
import math

import jax
import jax.numpy as jnp
from jax import lax
from jax.experimental import pallas as pl
from jax.experimental.pallas import tpu as pltpu
from jax.sharding import PartitionSpec as P

HEAD = 128
EPS = 1e-06
MASKED = -1e30
MESH = pl.DeviceIdType.MESH
BF = jnp.bfloat16
F32 = jnp.float32
NY = 4
NZ = 4
VMEM_LIMIT = 67_000_000


def spec(space):
    return pl.BlockSpec(memory_space=space)


def coords():
    d = lax.axis_index("dp")
    return d // (2 * NY), (d // 2) % NY, d % 2


def dp_of(xh, y, c):
    return (xh * NY + y) * 2 + c


def greet(peers):
    barrier = pltpu.get_barrier_semaphore()
    for peer in peers:
        pl.semaphore_signal(barrier, inc=1, device_id=peer, device_id_type=MESH)
    pl.semaphore_wait(barrier, len(peers))


def remote(src, dst, ssem, rsem, peer):
    return pltpu.make_async_remote_copy(
        src_ref=src, dst_ref=dst, send_sem=ssem, recv_sem=rsem, device_id=peer, device_id_type=MESH
    )


def nt(a, b):
    return lax.dot_general(a, b, (((1,), (1,)), ((), ())), preferred_element_type=F32)


def tn(a, b):
    return lax.dot_general(a, b, (((0,), (0,)), ((), ())), preferred_element_type=F32)


def fused_kernel(
    len_ref, hid_in, cot_in, gain_ref, wf_in, ws_in,
    res_out, states_out, dw0_out, dw1_out, gain_out,
    w, act, acc, proj, grads, give, wgt,
    dwb, rp, rf, rn, xs, xr, zp, zf, zn, zs, hid, gz, gs,
    asem, arsem, bsem, brsem, psem, prsem, fsem, frsem, nsem, nrsem, xsem, xrsem,
    zsem, zrsem, gsem, grsem, lsem,
):
    sec = lax.axis_index("section")
    z = lax.axis_index("mp")
    xh, y, c = coords()
    oh = 1 - xh
    yp, ym, yf = (y + 1) % NY, (y + 3) % NY, (y + 2) % NY
    zup, zdn, zfar = (z + 1) % NZ, (z + 3) % NZ, (z + 2) % NZ
    depth, columns = rp.shape[2:]
    half = depth // 2
    pair = 2 * depth
    length, width = act.shape[1:]
    rows = length // NZ
    hrows = rows // 2
    heads = columns // HEAD
    scale = 1.0 / math.sqrt(HEAD)
    sources = (wf_in, ws_in)
    outs = (res_out, states_out)
    dw_outs = (dw0_out, dw1_out)
    block = 16

    partner = {"dp": dp_of(xh, y, 1 - c)}
    xpeer = {"dp": dp_of(oh, y, c)}
    up = {"dp": dp_of(xh, yp, c)}
    down = {"dp": dp_of(xh, ym, c)}
    yfar = {"dp": dp_of(xh, yf, c)}
    above = {"mp": zup}
    below = {"mp": zdn}
    zopp = {"mp": zfar}
    other = {"section": 1 - sec}

    low, high = pl.ds(0, half), pl.ds(half, half)
    kinds = (
        ((xh, y), None, xpeer),
        ((xh, y), None, up),
        ((xh, y), None, down),
        ((oh, y), None, up),
        ((oh, y), None, down),
        ((xh, ym), low, up),
        ((xh, yp), high, down),
        ((oh, ym), low, up),
        ((oh, yp), high, down),
        ((xh, y), None, partner),
        ((oh, y), None, partner),
        ((xh, ym), None, partner),
        ((xh, yp), None, partner),
        ((oh, ym), None, partner),
        ((oh, yp), None, partner),
        ((xh, yf), None, partner),
        ((oh, yf), None, partner),
    )
    own = (0, 1, 2, 9)

    def message(t, k):
        (h, yy), part, peer = kinds[k]
        place = w.at[t, h * NY + yy, c]
        if part is not None:
            place = w.at[t, h * NY + yy, c, part]
        src = sources[t] if k in own else place
        return remote(src, place, asem.at[t, k], arsem.at[t, k], peer)

    def start(t, *ks):
        for k in ks:
            message(t, k).start()

    def arrived(t, *ks):
        for k in ks:
            message(t, k).wait_recv()

    def use(t, h, yy, first=False):
        p = h * NY + yy
        cols = pl.ds(pl.multiple_of(p * pair, 128), pair)
        left = act[0, :, cols] if t == 0 else act[sec, :, cols]
        part = jnp.dot(left, w[t, p].reshape(pair, columns), preferred_element_type=F32)
        if first:
            acc[t, pl.ds(0, length)] = part
        else:
            acc[t, pl.ds(0, length)] += part

    def head(h):
        return pl.ds(h * HEAD, HEAD)

    def forward(h, i):
        return remote(
            proj.at[i, :, head(h)], grads.at[0, i, :, head(h)], bsem.at[i, h], brsem.at[i, h], other
        )

    def backward(h, i):
        return remote(
            give.at[i, :, head(h)], grads.at[0, i, :, head(h)], bsem.at[i, h], brsem.at[i, h], other
        )

    def to_partner(t, p):
        return remote(dwb.at[t, p, 1 - c], rp.at[t, p], psem.at[t, p], prsem.at[t, p], partner)

    def far_message(t, h, way):
        hh = oh if h == 0 else xh
        part = pl.ds(way * half, half)
        return remote(
            rp.at[t, hh * NY + yf, part], rf.at[t, h, way], fsem.at[t, h, way], frsem.at[t, h, way],
            up if way == 0 else down,
        )

    def near_message(t, h, way):
        hh = oh if h == 0 else xh
        return remote(
            rp.at[t, hh * NY + (yp if way == 0 else ym)], rn.at[t, h, way],
            nsem.at[t, h, way], nrsem.at[t, h, way], up if way == 0 else down,
        )

    def x_message(t):
        return remote(xs.at[t], xr.at[t], xsem.at[t], xrsem.at[t], xpeer)

    def products(t, h, first, last):
        hh = oh if h == 0 else xh

        def body(j, carry):
            p = hh * NY + (y + 2 + j) % NY
            left = act[t * sec, :, pl.ds(pl.multiple_of(p * pair, 128), pair)]
            dwb[t, p] = tn(left, grads[sec, t]).astype(BF).reshape(2, depth, columns)
            to_partner(t, p).start()
            return carry

        lax.fori_loop(first, last, body, 0)

    def pair_sum(t, p, part=None):
        if part is None:
            part = pl.ds(0, depth)
        return dwb[t, p, c, part].astype(F32) + rp[t, p, part].astype(F32)

    def send_far(t, h):
        hh = oh if h == 0 else xh
        p = hh * NY + yf
        to_partner(t, p).wait_recv()
        rp[t, p] = pair_sum(t, p).astype(BF)
        far_message(t, h, 0).start()
        far_message(t, h, 1).start()

    def send_near(t, h):
        hh = oh if h == 0 else xh
        for way, yy in ((0, yp), (1, ym)):
            p = hh * NY + yy
            to_partner(t, p).wait_recv()
            far_message(t, h, way).wait_recv()
            mine, rest = pl.ds(way * half, half), pl.ds((1 - way) * half, half)
            rp[t, p, mine] = (pair_sum(t, p, mine) + rf[t, h, way].astype(F32)).astype(BF)
            rp[t, p, rest] = pair_sum(t, p, rest).astype(BF)
            near_message(t, h, way).start()

    def ring_total(t, h):
        hh = oh if h == 0 else xh
        p = hh * NY + y
        to_partner(t, p).wait_recv()
        near_message(t, h, 0).wait_recv()
        near_message(t, h, 1).wait_recv()
        return pair_sum(t, p) + rn[t, h, 0].astype(F32) + rn[t, h, 1].astype(F32)

    def send_x(t):
        xs[t] = ring_total(t, 0).astype(BF)
        x_message(t).start()

    def dw_copy(t):
        return pltpu.make_async_copy(acc.at[t], dw_outs[t], lsem.at[6 + t])

    def finish_dw(t):
        total = ring_total(t, 1)
        x_message(t).wait_recv()
        acc[t] = total + xr[t].astype(F32)
        dw_copy(t).start()

    def z_rows(who, part=None):
        if part is None:
            return pl.ds(pl.multiple_of(who * rows, rows), rows)
        return pl.ds(pl.multiple_of(who * rows + part * hrows, hrows), hrows)

    def z_far(a, way):
        return remote(
            zp.at[a, z_rows(zfar, way)], zf.at[a, way], zsem.at[a, way], zrsem.at[a, way],
            above if way == 0 else below,
        )

    def z_near(a, way):
        return remote(
            zp.at[a, z_rows(zup if way == 0 else zdn)], zn.at[a, way], zsem.at[a, 2 + way],
            zrsem.at[a, 2 + way], above if way == 0 else below,
        )

    def z_own(a, way):
        return remote(
            zs.at[a], outs[a].at[z_rows(z)], zsem.at[a, 4 + way], zrsem.at[a, 4 + way],
            above if way == 0 else below,
        )

    def z_pass(a, way):
        place = outs[a].at[z_rows(zdn if way == 0 else zup, way)]
        return remote(
            place, place, zsem.at[a, 6 + way], zrsem.at[a, 6 + way], above if way == 0 else below
        )

    def z_keep(a):
        return pltpu.make_async_copy(zs.at[a], outs[a].at[z_rows(z)], lsem.at[4 + a])

    def head_product(a, terms):
        def body(p, carry):
            total = None
            for t in terms:
                part = nt(grads[sec, t], w[t, p].reshape(pair, columns))
                total = part if total is None else total + part
            zp[a, :, pl.ds(pl.multiple_of(p * pair, 128), pair)] = total.astype(BF)
            return carry

        lax.fori_loop(0, 2 * NY, body, 0)
        z_far(a, 0).start()
        z_far(a, 1).start()

    def z_send_near(a):
        for way, who in ((0, zup), (1, zdn)):
            z_far(a, way).wait_recv()
            place = z_rows(who, way)
            zp[a, place] = (zp[a, place].astype(F32) + zf[a, way].astype(F32)).astype(BF)
            z_near(a, way).start()

    def z_total(a, r):
        return (
            zp[a, pl.ds(pl.multiple_of(z * rows + r, block), block)].astype(F32)
            + zn[a, 0, pl.ds(r, block)].astype(F32)
            + zn[a, 1, pl.ds(r, block)].astype(F32)
        )

    def z_spread(a):
        z_own(a, 0).start()
        z_own(a, 1).start()
        z_keep(a).start()

    def z_forward(a):
        for way in range(2):
            z_own(a, way).wait_recv()
            z_pass(a, way).start()

    def finish_output():
        z_near(0, 0).wait_recv()
        z_near(0, 1).wait_recv()

        def body(i, carry):
            r = pl.multiple_of(i * block, block)
            zs[0, pl.ds(r, block)] = (z_total(0, r) + hid[pl.ds(r, block)].astype(F32)).astype(BF)
            return carry

        lax.fori_loop(0, rows // block, body, 0)
        z_spread(0)

    def finish_states():
        z_near(1, 0).wait_recv()
        z_near(1, 1).wait_recv()
        gains = gain_ref[...]

        def body(i, carry):
            r = pl.multiple_of(i * block, block)
            wide = hid[pl.ds(r, block)].astype(F32)
            inverse = lax.rsqrt(jnp.mean(wide * wide, axis=-1, keepdims=True) + EPS)
            unit = wide * inverse
            extra = act[1, pl.ds(pl.multiple_of(z * rows + r, block), block)].astype(F32)
            grad = z_total(1, r) + jnp.where(sec == 0, extra, 0.0)
            scaled = grad * gains
            inner = jnp.mean(scaled * unit, axis=-1, keepdims=True)
            states = inverse * (scaled - unit * inner) + jnp.where(sec == 0, 0.0, extra)
            zs[1, pl.ds(r, block)] = states.astype(BF)
            gs[pl.ds(0, 1)] += jnp.sum(grad * unit, axis=0, keepdims=True)
            return carry

        gs[pl.ds(0, 1)] = jnp.zeros((1, width), F32)
        lax.fori_loop(0, rows // block, body, 0)
        for i in range(3):
            gain_message(i, 0).start()
        z_spread(1)

    gain_peers = (above, below, zopp, partner, xpeer, up, down, yfar)

    def gain_message(i, level):
        return remote(
            gs.at[pl.ds(level, 1)], gz.at[pl.ds(i, 1)], gsem.at[i], grsem.at[i], gain_peers[i]
        )

    gain_steps = (((0, 1, 2), 0), ((3,), 1), ((4,), 2), ((5, 6, 7), 3))

    def gain_step(level):
        slots, _ = gain_steps[level]
        total = gs[pl.ds(level, 1)]
        for i in slots:
            gain_message(i, level).wait_recv()
            total = total + gz[pl.ds(i, 1)]
        if level == 3:
            gain_out[...] = total
            return
        gs[pl.ds(level + 1, 1)] = total
        for i in gain_steps[level + 1][0]:
            gain_message(i, level + 1).start()

    def encoder_tail():
        for h in range(heads):
            forward(h, 1).start()
        for h in range(heads):
            backward(h, 1).wait_recv()
        products(1, 0, 0, 2)
        send_far(1, 0)
        products(1, 0, 2, 4)
        products(1, 1, 0, 2)
        send_far(1, 1)
        products(1, 1, 2, 4)
        for h in range(heads):
            backward(h, 0).wait_recv()
        products(0, 0, 0, 2)
        send_far(0, 0)
        head_product(1, (0, 1))
        send_near(1, 0)
        products(0, 0, 2, 4)
        products(0, 1, 0, 2)
        send_far(0, 1)
        send_near(0, 0)
        products(0, 1, 2, 4)
        z_send_near(1)
        send_x(1)
        send_near(1, 1)
        send_x(0)
        send_near(0, 1)
        finish_states()
        z_forward(1)
        gain_step(0)
        gain_step(1)
        finish_dw(1)
        gain_step(2)
        finish_dw(0)
        gain_step(3)

    def softmax_part():
        visible = lax.broadcasted_iota(jnp.int32, (1, length), 1) < len_ref[0, 0]
        for h in range(heads):
            forward(h, 0).wait_recv()
            scores = nt(proj[0, :, head(h)], grads[0, 0, :, head(h)]) * scale
            scores = jnp.where(visible, scores, MASKED)
            e = jnp.exp(scores - jnp.max(scores, axis=-1, keepdims=True))
            wgt[h] = e / jnp.sum(e, axis=-1, keepdims=True)

    def decoder_tail():
        for h in range(heads):
            give[1, :, head(h)] = tn(wgt[h].astype(BF), proj[1, :, head(h)]).astype(BF)
            backward(h, 1).start()
        for h in range(heads):
            forward(h, 1).wait_recv()
            weights = wgt[h]
            v = grads[0, 1, :, head(h)]
            grad_weights = nt(proj[1, :, head(h)], v)
            inner = jnp.sum(weights * grad_weights, axis=-1, keepdims=True)
            grad_scores = (weights * (grad_weights - inner) * scale).astype(BF)
            give[0, :, head(h)] = tn(grad_scores, proj[0, :, head(h)]).astype(BF)
            backward(h, 0).start()
            grads[1, 1, :, head(h)] = jnp.dot(
                weights.astype(BF), v, preferred_element_type=F32
            ).astype(BF)
            grads[1, 0, :, head(h)] = jnp.dot(
                grad_scores, grads[0, 0, :, head(h)], preferred_element_type=F32
            ).astype(BF)
        head_product(0, (1,))
        products(1, 0, 0, 1)
        products(0, 0, 0, 1)
        send_far(1, 0)
        send_far(0, 0)
        head_product(1, (0,))
        products(1, 0, 1, 4)
        z_send_near(0)
        products(0, 0, 1, 4)
        send_near(1, 0)
        send_near(0, 0)
        products(1, 1, 0, 1)
        products(0, 1, 0, 1)
        send_far(1, 1)
        send_far(0, 1)
        z_send_near(1)
        products(1, 1, 1, 4)
        products(0, 1, 1, 4)
        finish_output()
        send_x(1)
        send_x(0)
        send_near(1, 1)
        send_near(0, 1)
        finish_states()
        z_forward(0)
        gain_step(0)
        gain_step(1)
        finish_dw(1)
        gain_step(2)
        finish_dw(0)
        gain_step(3)
        z_forward(1)

    hid_all = pltpu.make_async_copy(hid_in, zp.at[0], lsem.at[0])
    cot_copy = pltpu.make_async_copy(cot_in, act.at[1], lsem.at[1])
    own_copy = [
        pltpu.make_async_copy(sources[t], w.at[t, xh * NY + y, c], lsem.at[2 + t]) for t in range(2)
    ]
    hid_copy = pltpu.make_async_copy(
        hid_in.at[z_rows(z)], hid, lsem.at[8]
    )
    hid_all.start()
    cot_copy.start()
    for copy in own_copy:
        copy.start()
    hid_copy.start()
    greet([partner, xpeer, up, down, yfar, above, below, zopp, other])
    start(0, 0, 1, 2, 9)
    start(1, 0, 9)

    hid_all.wait()
    cot_copy.wait()
    target_count = len_ref[0, 1]

    def norm_rows(i, carry):
        r = pl.ds(pl.multiple_of(i * block, block), block)
        wide = zp[0, r, :].astype(F32)
        inverse = lax.rsqrt(jnp.mean(wide * wide, axis=-1, keepdims=True) + EPS)
        act[0, r, :] = (wide * inverse * gain_ref[...]).astype(BF)
        row = i * block + lax.broadcasted_iota(jnp.int32, (block, 1), 0)
        keep = jnp.logical_or(row < target_count, sec == 0)
        act[1, r, :] = jnp.where(keep, act[1, r, :].astype(F32), 0.0).astype(BF)
        return carry

    lax.fori_loop(0, length // block, norm_rows, 0)
    for copy in own_copy:
        copy.wait()
    hid_copy.wait()

    memory_copy = pltpu.make_async_copy(act.at[0], res_out, lsem.at[9])

    @pl.when(sec == 0)
    def _():
        memory_copy.start()

    arrived(0, 1)
    start(0, 5, 11)
    arrived(0, 2)
    start(0, 6, 12)
    start(1, 1, 2)
    arrived(0, 9)
    use(0, xh, y, True)
    arrived(1, 9)
    use(1, xh, y, True)
    arrived(0, 0)
    start(0, 3, 4, 10)
    arrived(0, 11)
    use(0, xh, ym)
    arrived(0, 12)
    use(0, xh, yp)
    arrived(0, 5, 6)
    start(0, 15)
    arrived(0, 10)
    use(0, oh, y)
    arrived(1, 1)
    start(1, 5, 11)
    arrived(1, 2)
    start(1, 6, 12)
    arrived(0, 15)
    use(0, xh, yf)
    arrived(1, 0)
    start(1, 3, 4, 10)
    arrived(0, 3)
    start(0, 7, 13)
    arrived(0, 4)
    start(0, 8, 14)
    arrived(1, 11)
    use(1, xh, ym)
    arrived(1, 12)
    use(1, xh, yp)
    arrived(0, 13)
    use(0, oh, ym)
    arrived(0, 14)
    use(0, oh, yp)
    arrived(0, 7, 8)
    start(0, 16)
    arrived(1, 10)
    use(1, oh, y)
    arrived(1, 5, 6)
    start(1, 15)
    arrived(0, 16)
    use(0, oh, yf)
    proj[0] = acc[0, pl.ds(0, length)].astype(BF)

    @pl.when(sec == 0)
    def _():
        for h in range(heads):
            forward(h, 0).start()

    arrived(1, 15)
    use(1, xh, yf)
    arrived(1, 3)
    start(1, 7, 13)
    arrived(1, 4)
    start(1, 8, 14)
    arrived(1, 13)
    use(1, oh, ym)
    arrived(1, 14)
    use(1, oh, yp)

    @pl.when(sec == 1)
    def _():
        softmax_part()

    arrived(1, 7, 8)
    start(1, 16)
    arrived(1, 16)
    use(1, oh, yf)
    proj[1] = acc[1, pl.ds(0, length)].astype(BF)

    @pl.when(sec == 0)
    def _():
        encoder_tail()

    @pl.when(sec == 1)
    def _():
        decoder_tail()

    @pl.when(sec == 0)
    def _():
        memory_copy.wait()
        for h in range(heads):
            for i in range(2):
                forward(h, i).wait_send()

    @pl.when(sec == 1)
    def _():
        for h in range(heads):
            for i in range(2):
                backward(h, i).wait_send()
        z_keep(0).wait()
        for way in range(2):
            z_pass(0, way).wait_recv()
            for make in (z_far, z_near, z_own, z_pass):
                make(0, way).wait_send()

    for t in range(2):
        for k in range(len(kinds)):
            message(t, k).wait_send()
    z_keep(1).wait()
    for way in range(2):
        z_pass(1, way).wait_recv()
        for make in (z_far, z_near, z_own, z_pass):
            make(1, way).wait_send()
    for slots, level in gain_steps:
        for i in slots:
            gain_message(i, level).wait_send()
    for t in range(2):
        dw_copy(t).wait()
        x_message(t).wait_send()
        for h in range(2):
            for way in range(2):
                far_message(t, h, way).wait_send()
                near_message(t, h, way).wait_send()

    def drain(j, carry):
        to_partner(j % 2, j // 2).wait_send()
        return carry

    lax.fori_loop(0, 4 * NY, drain, 0)


def fused_call(lengths, hidden, cotangent, gain, w_first, w_second):
    length, width = hidden.shape
    depth, columns = w_first.shape
    heads = columns // HEAD
    rows = length // NZ
    dma = pltpu.SemaphoreType.DMA
    return pl.pallas_call(
        fused_kernel,
        out_shape=(
            jax.ShapeDtypeStruct((length, width), BF),
            jax.ShapeDtypeStruct((length, width), BF),
            jax.ShapeDtypeStruct((depth, columns), F32),
            jax.ShapeDtypeStruct((depth, columns), F32),
            jax.ShapeDtypeStruct((1, width), F32),
        ),
        in_specs=[
            spec(pltpu.SMEM), spec(pl.ANY), spec(pl.ANY), spec(pltpu.VMEM), spec(pl.ANY), spec(pl.ANY),
        ],
        out_specs=(spec(pl.ANY), spec(pl.ANY), spec(pl.ANY), spec(pl.ANY), spec(pltpu.VMEM)),
        scratch_shapes=[
            pltpu.VMEM((2, 2 * NY, 2, depth, columns), BF),
            pltpu.VMEM((2, length, width), BF),
            pltpu.VMEM((2, depth, columns), F32),
            pltpu.VMEM((2, length, columns), BF),
            pltpu.VMEM((2, 2, length, columns), BF),
            pltpu.VMEM((2, length, columns), BF),
            pltpu.VMEM((heads, length, length), F32),
            pltpu.VMEM((2, 2 * NY, 2, depth, columns), BF),
            pltpu.VMEM((2, 2 * NY, depth, columns), BF),
            pltpu.VMEM((2, 2, 2, depth // 2, columns), BF),
            pltpu.VMEM((2, 2, 2, depth, columns), BF),
            pltpu.VMEM((2, depth, columns), BF),
            pltpu.VMEM((2, depth, columns), BF),
            pltpu.VMEM((2, length, width), BF),
            pltpu.VMEM((2, 2, rows // 2, width), BF),
            pltpu.VMEM((2, 2, rows, width), BF),
            pltpu.VMEM((2, rows, width), BF),
            pltpu.VMEM((rows, width), BF),
            pltpu.VMEM((8, width), F32),
            pltpu.VMEM((8, width), F32),
            dma((2, 17)), dma((2, 17)),
            dma((2, heads)), dma((2, heads)),
            dma((2, 2 * NY)), dma((2, 2 * NY)),
            dma((2, 2, 2)), dma((2, 2, 2)),
            dma((2, 2, 2)), dma((2, 2, 2)),
            dma((2,)), dma((2,)),
            dma((2, 8)), dma((2, 8)),
            dma((8,)), dma((8,)),
            dma((10,)),
        ],
        compiler_params=pltpu.CompilerParams(
            collective_id=0, has_side_effects=True, vmem_limit_bytes=VMEM_LIMIT
        ),
        name="fused_sublayer",
    )(lengths, hidden, cotangent, gain, w_first, w_second)


def shards(hidden, gain, w_first, w_second, lengths, cotangent):
    result, d_hidden, dw0, dw1, gain_sum = fused_call(
        lengths, hidden[0, 0], cotangent[0, 0], gain, w_first[0], w_second[0]
    )
    depth = w_first.shape[1]
    gain_part = lax.dynamic_slice(gain_sum, (0, lax.axis_index("dp") * depth), (1, depth))
    return (result[None, None], d_hidden[None, None], gain_part, dw0[None], dw1[None])


def solution(mesh):
    return jax.shard_map(
        shards,
        mesh=mesh,
        in_specs=(
            P("section", "dp", None, None),
            P("section", None),
            P("section", "dp", "mp"),
            P("section", "dp", "mp"),
            P("dp", None),
            P("section", "dp", None, None),
        ),
        out_specs=(
            P("section", "dp", None, None),
            P("section", "dp", None, None),
            P("section", "dp"),
            P("section", "dp", "mp"),
            P("section", "dp", "mp"),
        ),
        check_vma=False,
    )
```

time: 684 us -> 183 us (0.27)
  waiting for transfers between devices: 495 us -> 0 us
  Pallas kernels: 0 us -> 173 us
  blocking collectives: 68.5 us -> 0 us
  matrix products: 48.7 us -> 0 us
  other arithmetic: 29.1 us -> 0 us
  between operations: 14.6 us -> 0.65 us
  local copies, waits for them, and re-layouts: 17 us -> 8.37 us
  starting transfers between devices: 8.47 us -> 0 us
    psum x1 -> x0, waiting for transfers between devices: 195 us -> none  [total_features(): return lax.psum(partial_value, 'mp')]
    pallas_call x0 -> x1, Pallas kernels: none -> 173 us  [fused_call(): pl.pallas_call(fused_kernel, out_shape=(jax.ShapeDtypeStruct((length, wid...]
    reduce_scatter x2 -> x0, waiting for transfers between devices: 151 us -> none  [the longest x1 92.4 us: shards(): lax.psum_scatter(weight_second.astype(jnp.bfloat16), 'dp', scatter_dimens...]
    all_gather x2 -> x0, waiting for transfers between devices: 122 us -> none  [the longest x1 61.1 us: shards(): lax.all_gather(w_first[0], 'dp', axis=0, tiled=True)]
    unnamed x1 -> x0, blocking collectives: 68.5 us -> none
    dot_general x11 -> x0, matrix products: 47.1 us -> none  [the longest x2 12.9 us: contract_rows(): lax.dot_general(left, right, (((0,), (0,)), ((), ())), preferred_element_...]
    ppermute x4 -> x0, waiting for transfers between devices: 26 us -> none  [passed_along(): return lax.ppermute(shard, axis, pairs)]
    broadcast_in_dim x4 -> x0, other arithmetic: 9.24 us -> none  [the longest x1 5.28 us: shards(): result[None]]
  transfers between devices with their start and end apart: 9 -> 0, of which waited for: 8 -> 0; matrix products, arithmetic and copies ran while one was open for 6% -> 0% of each run, Pallas kernels for 0% -> 0%
where the time goes in v2:
time: 183 us; the launch traced here: 182 us
  Pallas kernels  173 us (95%)
  local copies, waits for them, and re-layouts  8.37 us (5%)
    pallas_call x1, Pallas kernels, fused_call(): pl.pallas_call(fused_kernel, out_shape=(jax.ShapeDtypeStruct((length, wid...  173 us
    unnamed x10, local copies, waits for them, and re-layouts  7.05 us

profile of v2, /device:TPU:2, one launch (start us, length us, event | category | flops | bytes accessed | tf_op | source)
XLA Modules:
  0.0 182.1 jit_solution(4056406103144040110)
XLA Ops:
  0.6 173.1 %fused_sublayer.1 = (bf16[256,5120]{1,0:T(8,128)(2,1)}, bf16[256,5120]{1,0:T(8,128)(2,1)}, f32[320,640]{1,0:T(8,128)}, f32[320,640]{1,0:T(8,128)}, f32[1,5120]{1,0:T(1,128)}) custom-call(s32[1,2]{1,0:T(1,128)} %len_ref.1, bf16[256,5120]{1,0:T(8,128)(2,1)} %bitcast.8, bf16[256,5120]{1,0:T(8,128)(2,1)} %bitcast.9, f32[1,5120]{1,0:T(1,128)} %gain_ref.1, ...), custom_call_target="tpu_custom_call" | custom-call | tf_op jit(solution)/shard_map/fused_sublayer/pallas_call | solution.py:631
  173.7 1.3 constant_dynamic-slice_fusion
  175.0 0.0 copy-start
  175.0 3.6 %copy.15 = bf16[1,1,256,5120]{3,2,1,0:T(8,128)(2,1)} copy(bf16[1,1,256,5120]{3,2,1,0:T(8,128)(2,1)} %bitcast.11) | data formatting | bytes 5242880
  178.6 0.0 copy-done
  178.6 0.0 copy-start.2
  178.6 0.0 copy-start.1
  178.6 1.5 copy.16
  180.1 0.2 copy-done.2
  180.3 0.9 copy.17
  181.2 0.0 copy-done.1
  181.2 0.9 copy.18
Async XLA Ops:
  175.0 3.6 %copy-start = (bf16[256,5120]{1,0:T(8,128)(2,1)S(1)}, bf16[256,5120]{1,0:T(8,128)(2,1)}, u32[]{:S(2)}) copy-start(bf16[256,5120]{1,0:T(8,128)(2,1)} %get-tuple-element.11) | copy-start | bytes 7864324
  178.6 1.7 copy-start.2
  178.6 2.6 %copy-start.1 = (f32[320,640]{1,0:T(8,128)S(1)}, f32[320,640]{1,0:T(8,128)}, u32[]{:S(2)}) copy-start(f32[320,640]{1,0:T(8,128)} %get-tuple-element.14) | copy-start | bytes 2457604

commit v3 on v2

--- a/solution.py
+++ b/solution.py
@@ -58,7 +58,7 @@
     w, act, acc, proj, grads, give, wgt,
     dwb, rp, rf, rn, xs, xr, zp, zf, zn, zs, hid, gz, gs,
     asem, arsem, bsem, brsem, psem, prsem, fsem, frsem, nsem, nrsem, xsem, xrsem,
-    zsem, zrsem, gsem, grsem, lsem,
+    zsem, zrsem, gsem, grsem, osem, orsem, lsem,
 ):
     sec = lax.axis_index("section")
     z = lax.axis_index("mp")
@@ -245,16 +245,50 @@
             zrsem.at[a, 2 + way], above if way == 0 else below,
         )
 
+    side = pl.ds(0, width // 2)
+
+    def z_cols(a):
+        return pl.ds(width // 2, width // 2) if a == 0 else pl.ds(0, width)
+
     def z_own(a, way):
         return remote(
-            zs.at[a], outs[a].at[z_rows(z)], zsem.at[a, 4 + way], zrsem.at[a, 4 + way],
+            zs.at[a, :, z_cols(a)], outs[a].at[z_rows(z), z_cols(a)], zsem.at[a, 4 + way], zrsem.at[a, 4 + way],
             above if way == 0 else below,
         )
 
     def z_pass(a, way):
-        place = outs[a].at[z_rows(zdn if way == 0 else zup, way)]
+        place = outs[a].at[z_rows(zdn if way == 0 else zup, way), z_cols(a)]
         return remote(
             place, place, zsem.at[a, 6 + way], zrsem.at[a, 6 + way], above if way == 0 else below
+        )
+
+    def side_give():
+        return remote(
+            zs.at[0, :, side], zp.at[0, z_rows(z), side], osem.at[0], orsem.at[0], other
+        )
+
+    def side_own(way):
+        place = zp.at[0, z_rows(z), side]
+        return remote(
+            place, place, osem.at[1 + way], orsem.at[1 + way], above if way == 0 else below
+        )
+
+    def side_pass(way):
+        place = zp.at[0, z_rows(zdn if way == 0 else zup, way), side]
+        return remote(
+            place, place, osem.at[3 + way], orsem.at[3 + way], above if way == 0 else below
+        )
+
+    def side_back(way):
+        r = z_rows(zdn if way == 0 else zup)
+        return remote(
+            zp.at[0, r, side], res_out.at[r, side], osem.at[5 + way], orsem.at[5 + way], other
+        )
+
+    def side_back_far(way):
+        r = z_rows(zfar, way)
+        return remote(
+            zp.at[0, r, side], res_out.at[r, side], osem.at[7 + way], orsem.at[7 + way], other
         )
 
     def z_keep(a):
@@ -307,6 +341,7 @@
             return carry
 
         lax.fori_loop(0, rows // block, body, 0)
+        side_give().start()
         z_spread(0)
 
     def finish_states():
@@ -385,9 +420,19 @@
         send_near(0, 1)
         finish_states()
         z_forward(1)
+        side_give().wait_recv()
+        side_own(0).start()
+        side_own(1).start()
         gain_step(0)
         gain_step(1)
+        for way in range(2):
+            side_own(way).wait_recv()
+            side_pass(way).start()
+            side_back(way).start()
         finish_dw(1)
+        for way in range(2):
+            side_pass(way).wait_recv()
+            side_back_far(way).start()
         gain_step(2)
         finish_dw(0)
         gain_step(3)
@@ -581,6 +626,9 @@
     @pl.when(sec == 0)
     def _():
         memory_copy.wait()
+        for way in range(2):
+            for make in (side_own, side_pass, side_back, side_back_far):
+                make(way).wait_send()
         for h in range(heads):
             for i in range(2):
                 forward(h, i).wait_send()
@@ -591,6 +639,10 @@
             for i in range(2):
                 backward(h, i).wait_send()
         z_keep(0).wait()
+        side_give().wait_send()
+        for way in range(2):
+            side_back(way).wait_recv()
+            side_back_far(way).wait_recv()
         for way in range(2):
             z_pass(0, way).wait_recv()
             for make in (z_far, z_near, z_own, z_pass):
@@ -670,6 +722,7 @@
             dma((2,)), dma((2,)),
             dma((2, 8)), dma((2, 8)),
             dma((8,)), dma((8,)),
+            dma((9,)), dma((9,)),
             dma((10,)),
         ],
         compiler_params=pltpu.CompilerParams(

time: 183 us -> 191 us (1.044)
  Pallas kernels: 173 us -> 182 us
    pallas_call x1, Pallas kernels: 173 us -> 182 us  [fused_call(): pl.pallas_call(fused_kernel, out_shape=(jax.ShapeDtypeStruct((length, wid...]
where the time goes in v3:
time: 191 us
  Pallas kernels  182 us (95%)
  local copies, waits for them, and re-layouts  8.37 us (4%)
    pallas_call x1, Pallas kernels, fused_call(): pl.pallas_call(fused_kernel, out_shape=(jax.ShapeDtypeStruct((length, wid...  182 us
    unnamed x10, local copies, waits for them, and re-layouts  7.05 us

profile of v3, /device:TPU:2, one launch (start us, length us, event | category | flops | bytes accessed | tf_op | source)
XLA Modules:
  0.0 191.2 jit_solution(4385596050803984320)
XLA Ops:
  0.6 182.1 %fused_sublayer.1 = (bf16[256,5120]{1,0:T(8,128)(2,1)}, bf16[256,5120]{1,0:T(8,128)(2,1)}, f32[320,640]{1,0:T(8,128)}, f32[320,640]{1,0:T(8,128)}, f32[1,5120]{1,0:T(1,128)}) custom-call(s32[1,2]{1,0:T(1,128)} %len_ref.1, bf16[256,5120]{1,0:T(8,128)(2,1)} %bitcast.8, bf16[256,5120]{1,0:T(8,128)(2,1)} %bitcast.9, f32[1,5120]{1,0:T(1,128)} %gain_ref.1, ...), custom_call_target="tpu_custom_call" | custom-call | tf_op jit(solution)/shard_map/fused_sublayer/pallas_call | solution.py:683
  182.8 1.3 constant_dynamic-slice_fusion
  184.1 0.0 copy-start
  184.1 3.6 %copy.15 = bf16[1,1,256,5120]{3,2,1,0:T(8,128)(2,1)} copy(bf16[1,1,256,5120]{3,2,1,0:T(8,128)(2,1)} %bitcast.11) | data formatting | bytes 5242880
  187.7 0.0 copy-done
  187.7 0.0 copy-start.2
  187.7 0.0 copy-start.1
  187.7 1.5 copy.16
  189.2 0.2 copy-done.2
  189.4 0.9 copy.17
  190.3 0.0 copy-done.1
  190.3 0.9 copy.18
Async XLA Ops:
  184.1 3.6 %copy-start = (bf16[256,5120]{1,0:T(8,128)(2,1)S(1)}, bf16[256,5120]{1,0:T(8,128)(2,1)}, u32[]{:S(2)}) copy-start(bf16[256,5120]{1,0:T(8,128)(2,1)} %get-tuple-element.11) | copy-start | bytes 7864324
  187.7 1.7 copy-start.2
  187.7 2.6 %copy-start.1 = (f32[320,640]{1,0:T(8,128)S(1)}, f32[320,640]{1,0:T(8,128)}, u32[]{:S(2)}) copy-start(f32[320,640]{1,0:T(8,128)} %get-tuple-element.14) | copy-start | bytes 2457604
